TPU v7x, 32 devices: a whole 2x2x4 slice. The times are simulated.
32 devices in a mesh: lat: 8 (over z, y), lon: 4 (over x, core).
Axes of the slice: x: 2, y: 2, z: 4, core: 2. Of those that a mesh axis runs over, the one named last changes fastest.
Arguments:
- grid_feat: bfloat16 [32768, 512], P(('lat', 'lon')), may hold values from -6 to 6
- mesh_feat: bfloat16 [2048, 512], P(('lat', 'lon')), may hold values from -6 to 6
- enc_send: int32 [32, 9, 256], P(('lat', 'lon')), may hold values from 0 to 1023
- enc_recv: int32 [32, 9, 256], P(('lat', 'lon')), may hold values from 0 to 63
- enc_count: int32 [32, 9], P(('lat', 'lon')), may hold values from 0 to 256, as said below
- dec_send: int32 [32, 9, 512], P(('lat', 'lon')), may hold values from 0 to 63
- dec_recv: int32 [32, 9, 512], P(('lat', 'lon')), may hold values from 0 to 1023
- dec_count: int32 [32, 9], P(('lat', 'lon')), may hold values from 0 to 512, as said below
- enc_src: bfloat16 [512, 512], replicated, may hold values from -0.25 to 0.25
- enc_dst: bfloat16 [512, 512], replicated, may hold values from -0.25 to 0.25
- enc_bias: float32 [512], replicated, may hold values from -3 to 3
- enc_out: bfloat16 [512, 512], replicated, may hold values from -0.03125 to 0.03125
- dec_src: bfloat16 [512, 512], replicated, may hold values from -0.25 to 0.25
- dec_dst: bfloat16 [512, 512], replicated, may hold values from -0.25 to 0.25
- dec_bias: float32 [512], replicated, may hold values from -3 to 3
- dec_out: bfloat16 [512, 512], replicated, may hold values from -0.1875 to 0.1875
- grid_cot: bfloat16 [32768, 512], P(('lat', 'lon')), may hold values from -6 to 6
Outputs:
- grid_new: bfloat16 [32768, 512], P(('lat', 'lon'))
- mesh_grad: bfloat16 [2048, 512], P(('lat', 'lon'))
- grid_grad: bfloat16 [32768, 512], P(('lat', 'lon'))
Inputs may be any that keep to these rules, and one draw needn't show every extreme that they name: `enc_send`: row of the grid device's own tile. `enc_recv`: row of the mesh tile of the block's neighbour. `enc_count`: live slots of each block; 0 where the neighbour would lie beyond a pole; block 4 (the device itself) is full, and in every draw some device receives full blocks from all its neighbours. `dec_send`: row of the mesh tile of the block's neighbour. `dec_recv`: row of the grid device's own tile. `dec_count`: live slots of each block; 0 where the neighbour would lie beyond a pole; block 4 (the device itself) is full, and in every draw some device sends full blocks to all its neighbours.
All inputs are finite; a program needn't handle non-finite values.
Results may differ from a plain program's by a relative error of at most 0.0086.
Values may be sent and summed in bfloat16 or wider, within the bound.
A program may use at most 128 MiB of HBM per device.

v0:
```python
import jax
import jax.numpy as jnp
from jax import lax
from jax.sharding import PartitionSpec as P


def padded(array, sides, width):
    for axis, dim in sides:
        peers, length = (lax.axis_size(axis), array.shape[dim])
        up = [(i, (i + 1) % peers) for i in range(peers)]
        down = [(j, i) for i, j in up]
        last = lax.slice_in_dim(array, length - width, length, axis=dim)
        initial = lax.slice_in_dim(array, 0, width, axis=dim)
        before = lax.ppermute(last, axis, up)
        after = lax.ppermute(initial, axis, down)
        array = jnp.concatenate([before, array, after], axis=dim)
    return array


def passed_along(array, axis, by):
    peers = lax.axis_size(axis)
    pairs = [(i, i + by) for i in range(peers) if 0 <= i + by < peers]
    return lax.ppermute(array, axis, pairs)


def shifted(block, axis, distance):
    devices = range(lax.axis_size(axis))
    route = [((i - distance) % len(devices), i) for i in devices]
    return lax.ppermute(block, axis, route)


def silu_slope(pre_act):
    squashed = jax.nn.sigmoid(pre_act)
    return squashed * (1.0 + pre_act * (1.0 - squashed))


def slot_keep(counts, capacity):
    slot_index = lax.broadcasted_iota(jnp.int32, (counts.shape[0], capacity), 1)
    return (slot_index < counts[:, None]).astype(jnp.float32)[..., None]


def one_hot_rows(indices, row_count):
    return (indices.reshape(1, -1) == lax.broadcasted_iota(jnp.int32, (row_count, 1), 0)).astype(
        jnp.bfloat16
    )


def block_rows(indices, row_count):
    block_base = lax.broadcasted_iota(jnp.int32, indices.shape, 0) * row_count
    return block_base + indices


def near_rows(local_tile, framing):
    framed = framing(local_tile.reshape((1, 1) + local_tile.shape))
    return framed.reshape((-1,) + local_tile.shape[1:])


def fold_home(partial_value, lat_move, lon_move):
    framed = partial_value.reshape((3, 3, -1) + partial_value.shape[1:])
    combined = framed[1] + lat_move(framed[0], -1) + lat_move(framed[2], 1)
    return combined[1] + lon_move(combined[0], -1) + lon_move(combined[2], 1)


def on_device(
    grid_feat,
    mesh_feat,
    enc_send,
    enc_recv,
    enc_count,
    dec_send,
    dec_recv,
    dec_count,
    enc_src,
    enc_dst,
    enc_bias,
    enc_out,
    dec_src,
    dec_dst,
    dec_bias,
    dec_out,
    grid_cot,
):
    grid_rows = grid_feat.shape[0]
    mesh_rows = mesh_feat.shape[0]
    feature_width = grid_feat.shape[1]
    enc_grid_rows = enc_send[0]
    enc_mesh_rows = enc_recv[0]
    enc_keep = slot_keep(enc_count[0], enc_send.shape[2])
    projected = jnp.dot(grid_feat, enc_src, preferred_element_type=jnp.float32).astype(jnp.bfloat16)
    outgoing = projected[enc_grid_rows]
    grid_table = one_hot_rows(enc_grid_rows, grid_rows)
    mesh_near = near_rows(mesh_feat, lambda framed: padded(framed, (("lat", 0), ("lon", 1)), 1))
    near_side = jnp.dot(mesh_near, enc_dst, preferred_element_type=jnp.float32)
    slot_targets = block_rows(enc_mesh_rows, mesh_rows)
    enc_pre = outgoing.astype(jnp.float32) + near_side[slot_targets] + enc_bias
    enc_message = (jax.nn.silu(enc_pre) * enc_keep).astype(jnp.bfloat16).reshape(-1, feature_width)
    target_table = one_hot_rows(slot_targets, 9 * mesh_rows)
    enc_partial = jnp.dot(target_table, enc_message, preferred_element_type=jnp.float32)
    enc_total = fold_home(
        enc_partial,
        lambda piece, offset: passed_along(piece, "lat", offset),
        lambda piece, offset: shifted(piece, "lon", offset),
    )
    enc_sum = enc_total.astype(jnp.bfloat16)
    mesh_new = (
        mesh_feat.astype(jnp.float32)
        + jnp.dot(enc_sum, enc_out, preferred_element_type=jnp.float32)
    ).astype(jnp.bfloat16)
    dec_keep = slot_keep(dec_count[0], dec_send.shape[2])
    dec_targets = block_rows(dec_send[0], mesh_rows)
    dec_grid_rows = dec_recv[0]
    dec_proj = jnp.dot(mesh_new, dec_src, preferred_element_type=jnp.float32).astype(jnp.bfloat16)
    dec_near = near_rows(dec_proj, lambda framed: padded(framed, (("lat", 0), ("lon", 1)), 1))
    grid_side = jnp.dot(grid_feat, dec_dst, preferred_element_type=jnp.float32)
    dec_pre = dec_near[dec_targets].astype(jnp.float32) + grid_side[dec_grid_rows] + dec_bias
    dec_message = (jax.nn.silu(dec_pre) * dec_keep).astype(jnp.bfloat16).reshape(-1, feature_width)
    dec_table = one_hot_rows(dec_grid_rows, grid_rows)
    dec_sum = jnp.dot(dec_table, dec_message, preferred_element_type=jnp.float32).astype(
        jnp.bfloat16
    )
    grid_new = (
        grid_feat.astype(jnp.float32)
        + jnp.dot(dec_sum, dec_out, preferred_element_type=jnp.float32)
    ).astype(jnp.bfloat16)
    grid_back = jnp.dot(grid_cot, dec_out.T, preferred_element_type=jnp.float32).astype(
        jnp.bfloat16
    )
    dec_grad = (
        (grid_back[dec_grid_rows].astype(jnp.float32) * silu_slope(dec_pre) * dec_keep)
        .astype(jnp.bfloat16)
        .reshape(-1, feature_width)
    )
    dec_local = jnp.dot(dec_table, dec_grad, preferred_element_type=jnp.float32).astype(
        jnp.bfloat16
    )
    dec_grid = jnp.dot(dec_local, dec_dst.T, preferred_element_type=jnp.float32)
    near_table = one_hot_rows(dec_targets, 9 * mesh_rows)
    dec_partial = jnp.dot(near_table, dec_grad, preferred_element_type=jnp.float32)
    mesh_total = fold_home(
        dec_partial,
        lambda piece, offset: passed_along(piece, "lat", offset),
        lambda piece, offset: shifted(piece, "lon", offset),
    ).astype(jnp.bfloat16)
    mesh_back = jnp.dot(mesh_total, dec_src.T, preferred_element_type=jnp.float32)
    enc_back = jnp.dot(
        mesh_back.astype(jnp.bfloat16), enc_out.T, preferred_element_type=jnp.float32
    ).astype(jnp.bfloat16)
    back_near = near_rows(enc_back, lambda framed: padded(framed, (("lat", 0), ("lon", 1)), 1))
    enc_grad = (
        (back_near[slot_targets].astype(jnp.float32) * silu_slope(enc_pre) * enc_keep)
        .astype(jnp.bfloat16)
        .reshape(-1, feature_width)
    )
    grid_total = jnp.dot(grid_table, enc_grad, preferred_element_type=jnp.float32).astype(
        jnp.bfloat16
    )
    enc_partial_grad = jnp.dot(target_table, enc_grad, preferred_element_type=jnp.float32)
    enc_local = fold_home(
        enc_partial_grad,
        lambda piece, offset: passed_along(piece, "lat", offset),
        lambda piece, offset: shifted(piece, "lon", offset),
    ).astype(jnp.bfloat16)
    mesh_grad = (
        mesh_back + jnp.dot(enc_local, enc_dst.T, preferred_element_type=jnp.float32)
    ).astype(jnp.bfloat16)
    enc_grid = jnp.dot(grid_total, enc_src.T, preferred_element_type=jnp.float32)
    grid_grad = (grid_cot.astype(jnp.float32) + dec_grid + enc_grid).astype(jnp.bfloat16)
    return (grid_new, mesh_grad, grid_grad)


def solution(mesh):
    placed = (
        P(("lat", "lon"), None),
        P(("lat", "lon"), None),
        P(("lat", "lon"), None, None),
        P(("lat", "lon"), None, None),
        P(("lat", "lon"), None),
        P(("lat", "lon"), None, None),
        P(("lat", "lon"), None, None),
        P(("lat", "lon"), None),
        P(),
        P(),
        P(),
        P(),
        P(),
        P(),
        P(),
        P(),
        P(("lat", "lon"), None),
    )
    return jax.shard_map(
        on_device,
        mesh=mesh,
        in_specs=placed,
        out_specs=(P(("lat", "lon"), None), P(("lat", "lon"), None), P(("lat", "lon"), None)),
        check_vma=False,
    )
```

profile of v0, /device:TPU:13, one launch (start us, length us, event | category | flops | bytes accessed | tf_op | source)
XLA Modules:
  0.0 225.4 jit_solution(11159712946868885150)
XLA Ops:
  0.9 2.1 collective-permute-start
  5.5 2.1 convolution_convert_fusion.1
  7.5 2.9 %convolution_convert_fusion = bf16[1024,512]{1,0:T(8,128)(2,1)} fusion(bf16[1024,512]{1,0:T(8,128)(2,1)} %param.33, bf16[512,512]{1,0:T(8,128)(2,1)S(1)} %copy-done), kind=kOutput, calls=%fused_computation.40 | convolution fusion | flops 537395200 | bytes 2621440 | tf_op jit(solution)/shard_map/dot_general | solution.py:125
  10.6 1.3 collective-permute-start.3
  11.9 1.2 collective-permute-start.2
  13.1 7.5 %gather_fusion = bf16[2304,512]{1,0:T(8,128)(2,1)} fusion(bf16[1024,512]{1,0:T(8,128)(2,1)S(1)} %convolution_convert_fusion.1, s32[3072]{0:T(1024)S(1)} %pad_clamp_fusion.3), kind=kCustom, calls=%fused_computation | custom fusion | bytes 4727808 | tf_op jit(solution)/shard_map/gather | solution.py:90
  21.2 6.9 %gather_fusion.1 = f32[2304,512]{1,0:T(8,128)} fusion(f32[576,512]{1,0:T(8,128)S(1)} %fusion.52, s32[3072]{0:T(1024)S(1)} %pad_clamp_fusion.2), kind=kCustom, calls=%fused_computation.1 | custom fusion | bytes 9446400 | tf_op jit(solution)/shard_map/gather | solution.py:95
  28.2 5.6 %fusion.10 = f32[576,512]{1,0:T(8,128)S(1)} fusion(s32[2304]{0:T(1024)S(1)} %add.189, f32[2304,512]{1,0:T(8,128)} %gather_fusion.1, bf16[2304,512]{1,0:T(8,128)(2,1)} %gather_fusion, f32[2304]{0:T(1024)S(1)} %reshape.285, f32[512]{0:T(512)S(1)} %copy-done.29), kind=kOutput, calls=%fused_computation.24 | convolution fusion | flops 1370898432 | bytes 8278016 | tf_op jit(solution)/shard_map/dot_general | solution.py:98
  34.8 2.2 collective-permute-start.5
  37.0 3.0 %collective-permute-start.4 = (f32[3,64,512]{2,1,0:T(8,128)}, f32[3,64,512]{2,1,0:T(8,128)}, u32[]{:S(2)}, u32[]{:S(2)}) collective-permute-start(f32[3,64,512]{2,1,0:T(8,128)} %bitcast.6), channel_id=1, source_target_pairs={{4,0},{8,4},{12,8},{16,12},{20,16},{24,20},{28,24},{5,1},{9,5},{13... | collective-permute-start | bytes 1179656 | tf_op jit(solution)/shard_map/ppermute | solution.py:23
  41.4 2.1 fusion.53
  43.5 12.7 %collective-permute-done.5 = f32[3,64,512]{2,1,0:T(8,128)} collective-permute-done((f32[3,64,512]{2,1,0:T(8,128)}, f32[3,64,512]{2,1,0:T(8,128)}, u32[]{:S(2)}, u32[]{:S(2)}) %collective-permute-start.5) | collective-permute-done | bytes 393248 | tf_op jit(solution)/shard_map/ppermute | solution.py:23
  56.1 1.2 add_add_fusion.4
  58.1 1.3 collective-permute-start.7
  60.1 1.5 collective-permute-done.7
  61.6 2.2 collective-permute-done.6
  63.8 1.4 fusion.22
  65.6 2.1 collective-permute-start.8
  68.5 1.4 collective-permute-done.9
  69.9 1.1 collective-permute-done.8
  72.2 1.2 collective-permute-start.10
  74.2 12.6 %gather_fusion.3 = f32[4608,512]{1,0:T(8,128)} fusion(f32[1024,512]{1,0:T(8,128)S(1)} %fusion.53, s32[5120]{0:T(1024)S(1)} %pad_clamp_fusion), kind=kCustom, calls=%fused_computation.3 | custom fusion | bytes 18892800 | tf_op jit(solution)/shard_map/gather | solution.py:115
  86.8 15.4 %gather_fusion.4 = bf16[4608,512]{1,0:T(8,128)(2,1)} fusion(bf16[1024,512]{1,0:T(8,128)(2,1)} %convolution_convert_fusion, s32[5120]{0:T(1024)S(1)} %pad_clamp_fusion), kind=kCustom, calls=%fused_computation.4 | custom fusion | bytes 9455616 | tf_op jit(solution)/shard_map/gather | solution.py:129
  102.3 1.1 pad_maximum_fusion.1
  103.4 13.8 %gather_fusion.2 = bf16[4608,512]{1,0:T(8,128)(2,1)} fusion(bf16[576,512]{1,0:T(8,128)(2,1)S(1)} %bitcast.91, s32[5120]{0:T(1024)S(1)} %pad_clamp_fusion.1), kind=kCustom, calls=%fused_computation.2 | custom fusion | bytes 9455616 | tf_op jit(solution)/shard_map/gather | solution.py:115
  117.2 9.0 %fusion.4 = bf16[4608,512]{1,0:T(8,128)(2,1)S(1)} fusion(bf16[4608,512]{1,0:T(8,128)(2,1)} %gather_fusion.4, f32[4608,512]{1,0:T(8,128)} %gather_fusion.3, bf16[4608,512]{1,0:T(8,128)(2,1)} %gather_fusion.2, f32[4608]{0:T(1024)S(1)} %reshape.286, f32[512]{0:T(512)S(1)} %copy-done.28), kind=kLoop, calls=%fused_computation.14 | loop fusion | flops 33030144 | bytes 23613440 | tf_op jit(solution)/shard_map/convert_element_type | solution.py:130
  126.2 2.9 %fusion.2 = f32[576,512]{1,0:T(8,128)S(1)} fusion(bf16[4608,512]{1,0:T(8,128)(2,1)S(1)} %fusion.4, s32[4608]{0:T(1024)S(1)} %add.214), kind=kOutput, calls=%fused_computation.10 | convolution fusion | flops 2720563200 | bytes 5916672 | tf_op jit(solution)/shard_map/dot_general | solution.py:138
  129.3 3.7 %collective-permute-start.13 = (f32[3,64,512]{2,1,0:T(8,128)S(1)}, f32[3,64,512]{2,1,0:T(8,128)S(1)}, u32[]{:S(2)}, u32[]{:S(2)}) collective-permute-start(f32[3,64,512]{2,1,0:T(8,128)S(1)} %bitcast.102), channel_id=1, source_target_pairs={{0,4},{4,8},{8,12},{12,16},{16,20},{20,24},{24,28},{1,5},{5,9},{9,... | collective-permute-start | bytes 1179656 | tf_op jit(solution)/shard_map/ppermute | solution.py:23
  133.0 1.9 collective-permute-start.12
  134.9 15.7 %collective-permute-done.13 = f32[3,64,512]{2,1,0:T(8,128)S(1)} collective-permute-done((f32[3,64,512]{2,1,0:T(8,128)S(1)}, f32[3,64,512]{2,1,0:T(8,128)S(1)}, u32[]{:S(2)}, u32[]{:S(2)}) %collective-permute-start.13) | collective-permute-done | bytes 393248 | tf_op jit(solution)/shard_map/ppermute | solution.py:23
  150.7 1.1 collective-permute-start.15
  151.8 1.9 collective-permute-done.15
  153.7 2.5 %collective-permute-done.14 = f32[64,512]{1,0:T(8,128)S(1)} collective-permute-done((f32[64,512]{1,0:T(8,128)S(1)}, f32[64,512]{1,0:T(8,128)S(1)}, u32[]{:S(2)}, u32[]{:S(2)}) %collective-permute-start.14) | collective-permute-done | bytes 131104 | tf_op jit(solution)/shard_map/ppermute | solution.py:29
  157.2 1.6 collective-permute-start.17
  160.5 1.3 collective-permute-done.17
  161.8 1.6 collective-permute-done.16
  163.9 1.4 collective-permute-start.18
  165.3 12.7 %add_convert_fusion.1 = bf16[1024,512]{1,0:T(8,128)(2,1)} fusion(bf16[1024,512]{1,0:T(8,128)(2,1)S(1)} %copy-done.13, bf16[512,512]{1,0:T(8,128)(2,1)S(1)} %copy-done, f32[4608,512]{1,0:T(8,128)} %gather_fusion.3, bf16[4608,512]{1,0:T(8,128)(2,1)} %gather_fusion.2, f32[4608]{0:T(1024)S(1)} %copy-done.17, f32[512]{0:T(512)S(1)} %copy-done.28, s32[4608]{0:T(1024)S(1)} %eq.56), kind=kOutput, calls=%fused_computation.35 | convolution fusion | flops 5396758528 | bytes 16816128 | tf_op jit(solution)/shard_map/dot_general | solution.py:123
  178.1 7.5 %gather_fusion.5 = bf16[2304,512]{1,0:T(8,128)(2,1)} fusion(bf16[576,512]{1,0:T(8,128)(2,1)S(1)} %bitcast.92, s32[3072]{0:T(1024)S(1)} %pad_clamp_fusion.2), kind=kCustom, calls=%fused_computation.5 | custom fusion | bytes 4727808 | tf_op jit(solution)/shard_map/gather | solution.py:150
  185.6 4.7 %fusion.12 = bf16[2304,512]{1,0:T(8,128)(2,1)S(1)} fusion(bf16[2304,512]{1,0:T(8,128)(2,1)} %gather_fusion.5, f32[2304,512]{1,0:T(8,128)} %gather_fusion.1, bf16[2304,512]{1,0:T(8,128)(2,1)S(1)} %copy-done.1, f32[2304]{0:T(1024)S(1)} %copy-done.22, f32[512]{0:T(512)S(1)} %copy-done.30), kind=kLoop, calls=%fused_computation.28 | loop fusion | flops 16515072 | bytes 11807744 | tf_op jit(solution)/shard_map/convert_element_type | solution.py:151
  190.4 1.5 fusion.9
  192.9 3.4 %collective-permute-start.21 = (f32[3,64,512]{2,1,0:T(8,128)}, f32[3,64,512]{2,1,0:T(8,128)}, u32[]{:S(2)}, u32[]{:S(2)}) collective-permute-start(f32[3,64,512]{2,1,0:T(8,128)} %bitcast.26), channel_id=1, source_target_pairs={{0,4},{4,8},{8,12},{12,16},{16,20},{20,24},{24,28},{1,5},{5,9},{9,... | collective-permute-start | bytes 1179656 | tf_op jit(solution)/shard_map/ppermute | solution.py:23
  196.3 2.3 %collective-permute-start.20 = (f32[3,64,512]{2,1,0:T(8,128)}, f32[3,64,512]{2,1,0:T(8,128)}, u32[]{:S(2)}, u32[]{:S(2)}) collective-permute-start(f32[3,64,512]{2,1,0:T(8,128)} %bitcast.25), channel_id=1, source_target_pairs={{4,0},{8,4},{12,8},{16,12},{20,16},{24,20},{28,24},{5,1},{9,5},{13... | collective-permute-start | bytes 1179656 | tf_op jit(solution)/shard_map/ppermute | solution.py:23
  198.6 9.4 %fusion.19 = f32[1024,512]{1,0:T(8,128)} fusion(bf16[512,512]{1,0:T(8,128)(2,1)} %param.30, bf16[4608,512]{1,0:T(8,128)(2,1)} %copy-done.2, s32[4608]{0:T(1024)S(1)} %eq.56), kind=kOutput, calls=%fused_computation.39 | convolution fusion | flops 5373952000 | bytes 7358464 | tf_op jit(solution)/shard_map/dot_general | solution.py:136
  208.0 6.6 %collective-permute-done.21 = f32[3,64,512]{2,1,0:T(8,128)} collective-permute-done((f32[3,64,512]{2,1,0:T(8,128)}, f32[3,64,512]{2,1,0:T(8,128)}, u32[]{:S(2)}, u32[]{:S(2)}) %collective-permute-start.21) | collective-permute-done | bytes 393248 | tf_op jit(solution)/shard_map/ppermute | solution.py:23
  214.6 1.2 add_add_fusion.2
  217.2 6.2 %add_convert_fusion = bf16[1024,512]{1,0:T(8,128)(2,1)} fusion(f32[1024,512]{1,0:T(8,128)} %fusion.19, bf16[1024,512]{1,0:T(8,128)(2,1)} %param.33, bf16[512,512]{1,0:T(8,128)(2,1)} %param.25, bf16[2304,512]{1,0:T(8,128)(2,1)S(1)} %copy-done.4, s32[2304]{0:T(1024)S(1)} %copy-done.25), kind=kOutput, calls=%fused_computation.34 | convolution fusion | flops 2957770752 | bytes 7087104 | tf_op jit(solution)/shard_map/dot_general | solution.py:166
  223.4 1.9 fusion.21
  (130 shorter events, 16.1 us)
Async XLA Ops:
  0.6 6.9 %copy-start = (bf16[512,512]{1,0:T(8,128)(2,1)S(1)}, bf16[512,512]{1,0:T(8,128)(2,1)}, u32[]{:S(2)}) copy-start(bf16[512,512]{1,0:T(8,128)(2,1)} %param.32) | copy-start | bytes 1572868
  0.6 9.9 %copy-start.14 = (bf16[64,512]{1,0:T(8,128)(2,1)S(1)}, bf16[64,512]{1,0:T(8,128)(2,1)}, u32[]{:S(2)}) copy-start(bf16[64,512]{1,0:T(8,128)(2,1)} %param.18) | copy-start | bytes 196612
  0.7 9.8 %copy-start.23 = (s32[1,9,256]{2,0,1:T(1,128)S(1)}, s32[1,9,256]{2,0,1:T(1,128)}, u32[]{:S(2)}) copy-start(s32[1,9,256]{2,0,1:T(1,128)} %param.19) | copy-start | bytes 27652
  0.7 9.9 %collective-permute-start.1 = (bf16[1,1,64,512]{3,2,1,0:T(8,128)(2,1)}, bf16[1,1,64,512]{3,2,1,0:T(8,128)(2,1)S(1)}, u32[]{:S(2)}, u32[]{:S(2)}) collective-permute-start(bf16[1,1,64,512]{3,2,1,0:T(8,128)(2,1)} %bitcast.97), channel_id=1, source_target_pairs={{4,0},{8,4},{12,8},{16,12},{20,16},{24,20},{28,24},{0,28},{5,1},{9... | collective-permute-start | bytes 196616 | tf_op jit(solution)/shard_map/ppermute | solution.py:15
  0.9 9.6 %collective-permute-start = (bf16[1,1,64,512]{3,2,1,0:T(8,128)(2,1)}, bf16[1,1,64,512]{3,2,1,0:T(8,128)(2,1)S(1)}, u32[]{:S(2)}, u32[]{:S(2)}) collective-permute-start(bf16[1,1,64,512]{3,2,1,0:T(8,128)(2,1)} %bitcast.98), channel_id=1, source_target_pairs={{0,4},{4,8},{8,12},{12,16},{16,20},{20,24},{24,28},{28,0},{1,5},{5... | collective-permute-start | bytes 196616 | tf_op jit(solution)/shard_map/ppermute | solution.py:14
  10.5 17.6 %copy-start.21 = (f32[2304]{0:T(1024)}, f32[2304]{0:T(1024)S(1)}, u32[]{:S(2)}) copy-start(f32[2304]{0:T(1024)S(1)} %reshape.285) | copy-start | bytes 27652
  10.6 17.6 %copy-start.26 = (s32[2304]{0:T(1024)}, s32[2304]{0:T(1024)S(1)}, u32[]{:S(2)}) copy-start(s32[2304]{0:T(1024)S(1)} %add.189) | copy-start | bytes 27652
  10.6 10.0 %collective-permute-start.3 = (bf16[3,1,64,512]{3,2,1,0:T(8,128)(2,1)S(1)}, bf16[3,1,64,512]{3,2,1,0:T(8,128)(2,1)S(1)}, u32[]{:S(2)}, u32[]{:S(2)}) collective-permute-start(bf16[3,1,64,512]{3,2,1,0:T(8,128)(2,1)S(1)} %pad_maximum_fusion.3), channel_id=1, source_target_pairs={{1,0},{2,1},{3,2},{0,3},{5,4},{6,5},{7,6},{4,7},{9,8},{10,9},{11,1... | collective-permute-start | bytes 589832 | tf_op jit(solution)/shard_map/ppermute | solution.py:15
  11.9 8.7 %collective-permute-start.2 = (bf16[3,1,64,512]{3,2,1,0:T(8,128)(2,1)S(1)}, bf16[3,1,64,512]{3,2,1,0:T(8,128)(2,1)S(1)}, u32[]{:S(2)}, u32[]{:S(2)}) collective-permute-start(bf16[3,1,64,512]{3,2,1,0:T(8,128)(2,1)S(1)} %pad_maximum_fusion.3), channel_id=1, source_target_pairs={{0,1},{1,2},{2,3},{3,0},{4,5},{5,6},{6,7},{7,4},{8,9},{9,10},{10,1... | collective-permute-start | bytes 589832 | tf_op jit(solution)/shard_map/ppermute | solution.py:14
  13.1 7.7 %copy-start.7 = (bf16[512,512]{1,0:T(8,128)(2,1)S(1)}, bf16[512,512]{1,0:T(8,128)(2,1)}, u32[]{:S(2)}) copy-start(bf16[512,512]{1,0:T(8,128)(2,1)} %param.26) | copy-start | bytes 1572868
  21.2 7.0 %copy-start.29 = (f32[512]{0:T(512)S(1)}, f32[512]{0:T(512)}, u32[]{:S(2)}) copy-start(f32[512]{0:T(512)} %param.27) | copy-start | bytes 6148
  28.2 11.9 %copy-start.19 = (s32[1,9,512]{2,0,1:T(1,128)S(1)}, s32[1,9,512]{2,0,1:T(1,128)}, u32[]{:S(2)}) copy-start(s32[1,9,512]{2,0,1:T(1,128)} %param.23) | copy-start | bytes 55300
  28.2 12.6 %copy-start.18 = (s32[1,9,512]{2,0,1:T(1,128)S(1)}, s32[1,9,512]{2,0,1:T(1,128)}, u32[]{:S(2)}) copy-start(s32[1,9,512]{2,0,1:T(1,128)} %param.22) | copy-start | bytes 55300
  33.8 30.0 %copy-start.5 = (bf16[512,512]{1,0:T(8,128)(2,1)S(1)}, bf16[512,512]{1,0:T(8,128)(2,1)}, u32[]{:S(2)}) copy-start(bf16[512,512]{1,0:T(8,128)(2,1)} %param.29) | copy-start | bytes 1572868
  34.8 21.4 %collective-permute-start.5 = (f32[3,64,512]{2,1,0:T(8,128)}, f32[3,64,512]{2,1,0:T(8,128)}, u32[]{:S(2)}, u32[]{:S(2)}) collective-permute-start(f32[3,64,512]{2,1,0:T(8,128)} %bitcast.7), channel_id=1, source_target_pairs={{0,4},{4,8},{8,12},{12,16},{16,20},{20,24},{24,28},{1,5},{5,9},{9,... | collective-permute-start | bytes 1179656 | tf_op jit(solution)/shard_map/ppermute | solution.py:23
  37.0 19.1 %collective-permute-start.4 = (f32[3,64,512]{2,1,0:T(8,128)}, f32[3,64,512]{2,1,0:T(8,128)}, u32[]{:S(2)}, u32[]{:S(2)}) collective-permute-start(f32[3,64,512]{2,1,0:T(8,128)} %bitcast.6), channel_id=1, source_target_pairs={{4,0},{8,4},{12,8},{16,12},{20,16},{24,20},{28,24},{5,1},{9,5},{13... | collective-permute-start | bytes 1179656 | tf_op jit(solution)/shard_map/ppermute | solution.py:23
  58.1 3.5 %collective-permute-start.7 = (f32[64,512]{1,0:T(8,128)S(1)}, f32[64,512]{1,0:T(8,128)S(1)}, u32[]{:S(2)}, u32[]{:S(2)}) collective-permute-start(f32[64,512]{1,0:T(8,128)S(1)} %get-tuple-element.17), channel_id=1, source_target_pairs={{3,0},{0,1},{1,2},{2,3},{7,4},{4,5},{5,6},{6,7},{11,8},{8,9},{9,10... | collective-permute-start | bytes 393224 | tf_op jit(solution)/shard_map/ppermute | solution.py:29
  59.4 4.4 %collective-permute-start.6 = (f32[64,512]{1,0:T(8,128)S(1)}, f32[64,512]{1,0:T(8,128)S(1)}, u32[]{:S(2)}, u32[]{:S(2)}) collective-permute-start(f32[64,512]{1,0:T(8,128)S(1)} %get-tuple-element.16), channel_id=1, source_target_pairs={{1,0},{2,1},{3,2},{0,3},{5,4},{6,5},{7,6},{4,7},{9,8},{10,9},{11,1... | collective-permute-start | bytes 393224 | tf_op jit(solution)/shard_map/ppermute | solution.py:29
  65.2 4.7 %collective-permute-start.9 = (bf16[1,1,64,512]{3,2,1,0:T(8,128)(2,1)S(1)}, bf16[1,1,64,512]{3,2,1,0:T(8,128)(2,1)S(1)}, u32[]{:S(2)}, u32[]{:S(2)}) collective-permute-start(bf16[1,1,64,512]{3,2,1,0:T(8,128)(2,1)S(1)} %fusion.22), channel_id=1, source_target_pairs={{4,0},{8,4},{12,8},{16,12},{20,16},{24,20},{28,24},{0,28},{5,1},{9... | collective-permute-start | bytes 196616 | tf_op jit(solution)/shard_map/ppermute | solution.py:15
  65.6 5.4 %collective-permute-start.8 = (bf16[1,1,64,512]{3,2,1,0:T(8,128)(2,1)S(1)}, bf16[1,1,64,512]{3,2,1,0:T(8,128)(2,1)S(1)}, u32[]{:S(2)}, u32[]{:S(2)}) collective-permute-start(bf16[1,1,64,512]{3,2,1,0:T(8,128)(2,1)S(1)} %fusion.22), channel_id=1, source_target_pairs={{0,4},{4,8},{8,12},{12,16},{16,20},{20,24},{24,28},{28,0},{1,5},{5... | collective-permute-start | bytes 196616 | tf_op jit(solution)/shard_map/ppermute | solution.py:14
  68.5 48.7 %copy-start.16 = (f32[4608]{0:T(1024)}, f32[4608]{0:T(1024)S(1)}, u32[]{:S(2)}) copy-start(f32[4608]{0:T(1024)S(1)} %reshape.286) | copy-start | bytes 55300
  71.7 30.6 %collective-permute-start.11 = (bf16[3,1,64,512]{3,2,1,0:T(8,128)(2,1)}, bf16[3,1,64,512]{3,2,1,0:T(8,128)(2,1)}, u32[]{:S(2)}, u32[]{:S(2)}) collective-permute-start(bf16[3,1,64,512]{3,2,1,0:T(8,128)(2,1)} %pad_maximum_fusion.4), channel_id=1, source_target_pairs={{1,0},{2,1},{3,2},{0,3},{5,4},{6,5},{7,6},{4,7},{9,8},{10,9},{11,1... | collective-permute-start | bytes 589832 | tf_op jit(solution)/shard_map/ppermute | solution.py:15
  72.2 30.1 %collective-permute-start.10 = (bf16[3,1,64,512]{3,2,1,0:T(8,128)(2,1)}, bf16[3,1,64,512]{3,2,1,0:T(8,128)(2,1)}, u32[]{:S(2)}, u32[]{:S(2)}) collective-permute-start(bf16[3,1,64,512]{3,2,1,0:T(8,128)(2,1)} %pad_maximum_fusion.4), channel_id=1, source_target_pairs={{0,1},{1,2},{2,3},{3,0},{4,5},{5,6},{6,7},{7,4},{8,9},{9,10},{10,1... | collective-permute-start | bytes 589832 | tf_op jit(solution)/shard_map/ppermute | solution.py:14
  86.8 15.4 %copy-start.15 = (s32[9,512]{1,0:T(8,128)S(1)}, s32[9,512]{1,0:T(8,128)}, u32[]{:S(2)}) copy-start(s32[9,512]{1,0:T(8,128)} %reduce.6) | copy-start | bytes 55300
  103.4 13.8 %copy-start.28 = (f32[512]{0:T(512)S(1)}, f32[512]{0:T(512)}, u32[]{:S(2)}) copy-start(f32[512]{0:T(512)} %param.31) | copy-start | bytes 6148
  129.2 27.4 %copy-start.6 = (bf16[512,512]{1,0:T(8,128)(2,1)S(1)}, bf16[512,512]{1,0:T(8,128)(2,1)}, u32[]{:S(2)}) copy-start(bf16[512,512]{1,0:T(8,128)(2,1)} %param.28) | copy-start | bytes 1572868
  129.2 30.6 %copy-start.20 = (s32[1,9,512]{2,0,1:T(1,128)S(1)}, s32[1,9,512]{2,0,1:T(1,128)}, u32[]{:S(2)}) copy-start(s32[1,9,512]{2,0,1:T(1,128)} %param.23) | copy-start | bytes 55300
  129.2 30.7 %copy-start.24 = (s32[1,9,256]{2,0,1:T(1,128)S(1)}, s32[1,9,256]{2,0,1:T(1,128)}, u32[]{:S(2)}) copy-start(s32[1,9,256]{2,0,1:T(1,128)} %param.19) | copy-start | bytes 27652
  129.2 36.1 %copy-start.13 = (bf16[1024,512]{1,0:T(8,128)(2,1)S(1)}, bf16[1024,512]{1,0:T(8,128)(2,1)}, u32[]{:S(2)}) copy-start(bf16[1024,512]{1,0:T(8,128)(2,1)} %param.17) | copy-start | bytes 3145732
  129.2 36.1 %copy-start.17 = (f32[4608]{0:T(1024)S(1)}, f32[4608]{0:T(1024)}, u32[]{:S(2)}) copy-start(f32[4608]{0:T(1024)} %copy-done.16) | copy-start | bytes 55300
  129.3 21.3 %collective-permute-start.13 = (f32[3,64,512]{2,1,0:T(8,128)S(1)}, f32[3,64,512]{2,1,0:T(8,128)S(1)}, u32[]{:S(2)}, u32[]{:S(2)}) collective-permute-start(f32[3,64,512]{2,1,0:T(8,128)S(1)} %bitcast.102), channel_id=1, source_target_pairs={{0,4},{4,8},{8,12},{12,16},{16,20},{20,24},{24,28},{1,5},{5,9},{9,... | collective-permute-start | bytes 1179656 | tf_op jit(solution)/shard_map/ppermute | solution.py:23
  133.0 17.6 %collective-permute-start.12 = (f32[3,64,512]{2,1,0:T(8,128)S(1)}, f32[3,64,512]{2,1,0:T(8,128)S(1)}, u32[]{:S(2)}, u32[]{:S(2)}) collective-permute-start(f32[3,64,512]{2,1,0:T(8,128)S(1)} %bitcast.101), channel_id=1, source_target_pairs={{4,0},{8,4},{12,8},{16,12},{20,16},{24,20},{28,24},{5,1},{9,5},{13... | collective-permute-start | bytes 1179656 | tf_op jit(solution)/shard_map/ppermute | solution.py:23
  150.7 3.0 %collective-permute-start.15 = (f32[64,512]{1,0:T(8,128)S(1)}, f32[64,512]{1,0:T(8,128)S(1)}, u32[]{:S(2)}, u32[]{:S(2)}) collective-permute-start(f32[64,512]{1,0:T(8,128)S(1)} %get-tuple-element.15), channel_id=1, source_target_pairs={{3,0},{0,1},{1,2},{2,3},{7,4},{4,5},{5,6},{6,7},{11,8},{8,9},{9,10... | collective-permute-start | bytes 393224 | tf_op jit(solution)/shard_map/ppermute | solution.py:29
  151.8 4.5 %collective-permute-start.14 = (f32[64,512]{1,0:T(8,128)S(1)}, f32[64,512]{1,0:T(8,128)S(1)}, u32[]{:S(2)}, u32[]{:S(2)}) collective-permute-start(f32[64,512]{1,0:T(8,128)S(1)} %get-tuple-element.14), channel_id=1, source_target_pairs={{1,0},{2,1},{3,2},{0,3},{5,4},{6,5},{7,6},{4,7},{9,8},{10,9},{11,1... | collective-permute-start | bytes 393224 | tf_op jit(solution)/shard_map/ppermute | solution.py:29
  157.2 4.6 %collective-permute-start.17 = (bf16[1,1,64,512]{3,2,1,0:T(8,128)(2,1)S(1)}, bf16[1,1,64,512]{3,2,1,0:T(8,128)(2,1)S(1)}, u32[]{:S(2)}, u32[]{:S(2)}) collective-permute-start(bf16[1,1,64,512]{3,2,1,0:T(8,128)(2,1)S(1)} %fusion.23), channel_id=1, source_target_pairs={{4,0},{8,4},{12,8},{16,12},{20,16},{24,20},{28,24},{0,28},{5,1},{9... | collective-permute-start | bytes 196616 | tf_op jit(solution)/shard_map/ppermute | solution.py:15
  158.8 4.7 %collective-permute-start.16 = (bf16[1,1,64,512]{3,2,1,0:T(8,128)(2,1)S(1)}, bf16[1,1,64,512]{3,2,1,0:T(8,128)(2,1)S(1)}, u32[]{:S(2)}, u32[]{:S(2)}) collective-permute-start(bf16[1,1,64,512]{3,2,1,0:T(8,128)(2,1)S(1)} %fusion.23), channel_id=1, source_target_pairs={{0,4},{4,8},{8,12},{12,16},{16,20},{20,24},{24,28},{28,0},{1,5},{5... | collective-permute-start | bytes 196616 | tf_op jit(solution)/shard_map/ppermute | solution.py:14
  163.5 14.5 %collective-permute-start.19 = (bf16[3,1,64,512]{3,2,1,0:T(8,128)(2,1)S(1)}, bf16[3,1,64,512]{3,2,1,0:T(8,128)(2,1)S(1)}, u32[]{:S(2)}, u32[]{:S(2)}) collective-permute-start(bf16[3,1,64,512]{3,2,1,0:T(8,128)(2,1)S(1)} %pad_maximum_fusion.5), channel_id=1, source_target_pairs={{1,0},{2,1},{3,2},{0,3},{5,4},{6,5},{7,6},{4,7},{9,8},{10,9},{11,1... | collective-permute-start | bytes 589832 | tf_op jit(solution)/shard_map/ppermute | solution.py:15
  163.9 14.1 %collective-permute-start.18 = (bf16[3,1,64,512]{3,2,1,0:T(8,128)(2,1)S(1)}, bf16[3,1,64,512]{3,2,1,0:T(8,128)(2,1)S(1)}, u32[]{:S(2)}, u32[]{:S(2)}) collective-permute-start(bf16[3,1,64,512]{3,2,1,0:T(8,128)(2,1)S(1)} %pad_maximum_fusion.5), channel_id=1, source_target_pairs={{0,1},{1,2},{2,3},{3,0},{4,5},{5,6},{6,7},{7,4},{8,9},{9,10},{10,1... | collective-permute-start | bytes 589832 | tf_op jit(solution)/shard_map/ppermute | solution.py:14
  178.1 7.6 %copy-start.1 = (bf16[2304,512]{1,0:T(8,128)(2,1)S(1)}, bf16[2304,512]{1,0:T(8,128)(2,1)}, u32[]{:S(2)}) copy-start(bf16[2304,512]{1,0:T(8,128)(2,1)} %gather_fusion) | copy-start | bytes 7077892
  178.1 7.5 %copy-start.22 = (f32[2304]{0:T(1024)S(1)}, f32[2304]{0:T(1024)}, u32[]{:S(2)}) copy-start(f32[2304]{0:T(1024)} %copy-done.21) | copy-start | bytes 27652
  178.1 7.5 %copy-start.30 = (f32[512]{0:T(512)S(1)}, f32[512]{0:T(512)}, u32[]{:S(2)}) copy-start(f32[512]{0:T(512)} %param.27) | copy-start | bytes 6148
  192.9 21.7 %collective-permute-start.21 = (f32[3,64,512]{2,1,0:T(8,128)}, f32[3,64,512]{2,1,0:T(8,128)}, u32[]{:S(2)}, u32[]{:S(2)}) collective-permute-start(f32[3,64,512]{2,1,0:T(8,128)} %bitcast.26), channel_id=1, source_target_pairs={{0,4},{4,8},{8,12},{12,16},{16,20},{20,24},{24,28},{1,5},{5,9},{9,... | collective-permute-start | bytes 1179656 | tf_op jit(solution)/shard_map/ppermute | solution.py:23
  196.2 20.9 %copy-start.4 = (bf16[2304,512]{1,0:T(8,128)(2,1)S(1)}, bf16[2304,512]{1,0:T(8,128)(2,1)}, u32[]{:S(2)}) copy-start(bf16[2304,512]{1,0:T(8,128)(2,1)} %copy-done.3) | copy-start | bytes 7077892
  196.3 20.9 %copy-start.25 = (s32[2304]{0:T(1024)S(1)}, s32[2304]{0:T(1024)}, u32[]{:S(2)}) copy-start(s32[2304]{0:T(1024)} %eq.66) | copy-start | bytes 27652
  196.3 18.3 %collective-permute-start.20 = (f32[3,64,512]{2,1,0:T(8,128)}, f32[3,64,512]{2,1,0:T(8,128)}, u32[]{:S(2)}, u32[]{:S(2)}) collective-permute-start(f32[3,64,512]{2,1,0:T(8,128)} %bitcast.25), channel_id=1, source_target_pairs={{4,0},{8,4},{12,8},{16,12},{20,16},{24,20},{28,24},{5,1},{9,5},{13... | collective-permute-start | bytes 1179656 | tf_op jit(solution)/shard_map/ppermute | solution.py:23
  216.6 6.8 %collective-permute-start.23 = (f32[64,512]{1,0:T(8,128)}, f32[64,512]{1,0:T(8,128)}, u32[]{:S(2)}, u32[]{:S(2)}) collective-permute-start(f32[64,512]{1,0:T(8,128)} %get-tuple-element.13), channel_id=1, source_target_pairs={{3,0},{0,1},{1,2},{2,3},{7,4},{4,5},{5,6},{6,7},{11,8},{8,9},{9,10... | collective-permute-start | bytes 393224 | tf_op jit(solution)/shard_map/ppermute | solution.py:29
  217.2 6.2 %copy-start.12 = (f32[64,512]{1,0:T(8,128)S(1)}, f32[64,512]{1,0:T(8,128)}, u32[]{:S(2)}) copy-start(f32[64,512]{1,0:T(8,128)} %copy-done.11) | copy-start | bytes 393220
  217.2 6.2 %collective-permute-start.22 = (f32[64,512]{1,0:T(8,128)}, f32[64,512]{1,0:T(8,128)}, u32[]{:S(2)}, u32[]{:S(2)}) collective-permute-start(f32[64,512]{1,0:T(8,128)} %get-tuple-element.12), channel_id=1, source_target_pairs={{1,0},{2,1},{3,2},{0,3},{5,4},{6,5},{7,6},{4,7},{9,8},{10,9},{11,1... | collective-permute-start | bytes 393224 | tf_op jit(solution)/shard_map/ppermute | solution.py:29
  (7 other events, 18.2 us)
where the time goes:
time: 229 us; the launch traced here: 225 us
  local copies, waits for them, and re-layouts  69.2 us (30%)
  matrix products  49.8 us (22%)
  waiting for transfers between devices  48.6 us (21%)
  starting transfers between devices  32.8 us (14%)
  other arithmetic  23.7 us (10%)
    ppermute x6, waiting for transfers between devices, passed_along(): return lax.ppermute(array, axis, pairs)  35 us
    ppermute x6, starting transfers between devices, passed_along(): return lax.ppermute(array, axis, pairs)  16.5 us
    gather x1, local copies, waits for them, and re-layouts, on_device(): grid_back[dec_grid_rows].astype(jnp.float32) * silu_slope(dec_pre)  15.4 us
    gather x1, local copies, waits for them, and re-layouts, on_device(): dec_near[dec_targets].astype(jnp.float32) + grid_side[dec_grid_rows]  13.8 us
    dot_general x1, matrix products, on_device(): jnp.dot(dec_sum, dec_out, preferred_element_type=jnp.float32)  12.7 us
    gather x1, local copies, waits for them, and re-layouts, on_device(): grid_side[dec_grid_rows]  12.6 us
    dot_general x1, matrix products, on_device(): dec_grid = jnp.dot(dec_local, dec_dst.T, preferred_element_type=jnp.float32)  9.38 us
    convert_element_type x1, other arithmetic, on_device(): dec_grad = (grid_back[dec_grid_rows].astype(jnp.float32) * silu_slope(dec...  9.02 us
  transfers between devices with their start and end apart: 24, of which 11 were waited for; matrix products, arithmetic and copies ran while one was open for 34% of the time, Pallas kernels for 0%

commit v1 on v0

v1 whole, which is shorter than its diff:
```python
import functools

import jax
import jax.numpy as jnp
from jax import lax
from jax.experimental import pallas as pl
from jax.experimental.pallas import tpu as pltpu
from jax.sharding import PartitionSpec as P

F32 = jnp.float32
BF16 = jnp.bfloat16
MESH = pl.DeviceIdType.MESH


def mm(a, b):
    return jnp.dot(a, b, preferred_element_type=F32)


def mm_t(a, b):
    return lax.dot_general(a, b, (((1,), (1,)), ((), ())), preferred_element_type=F32)


def lane_row(width):
    return lax.broadcasted_iota(jnp.int32, (1, width), 1)


def ones_where(mask):
    return jnp.where(mask, 1.0, 0.0).astype(BF16)


def pick_columns(column, row_count):
    return ones_where(column == lane_row(row_count).astype(F32))


def pick_rows(indices, row_count, base=0):
    rows = lax.broadcasted_iota(jnp.int32, (row_count, 1), 0) + base
    return ones_where(rows == indices)


def column_of(columns_ref, at):
    columns = columns_ref[...]
    lane = lax.broadcasted_iota(jnp.int32, columns.shape, 1)
    return jnp.sum(jnp.where(lane == at, columns, 0.0), axis=1, keepdims=True)


def live_row(index_ref, count_ref, k):
    indices = index_ref[pl.ds(k, 1), :]
    return jnp.where(lane_row(indices.shape[1]) < count_ref[0, k], indices, -1)


def gate_of(pre):
    return 0.5 * jnp.tanh(0.5 * pre) + 0.5


def kernel(
    n_lat,
    n_lon,
    grid_feat,
    mesh_feat,
    enc_send,
    enc_recv,
    enc_count,
    dec_send,
    dec_recv,
    dec_count,
    enc_columns,
    dec_columns,
    enc_src,
    enc_dst,
    enc_bias,
    enc_out,
    dec_src,
    dec_dst,
    dec_bias,
    dec_out,
    grid_cot,
    grid_new,
    mesh_grad,
    grid_grad,
    enc_table,
    dec_table,
    enc_edges,
    enc_slope,
    dec_edges,
    grid_part,
    mesh_back,
    tile_out,
    part_out,
    landed,
    send_sem,
    recv_sem,
):
    lat = lax.axis_index("lat")
    lon = lax.axis_index("lon")
    grid_rows, width = grid_feat.shape
    mesh_rows = mesh_feat.shape[0]
    enc_cap = enc_send.shape[1]
    dec_cap = dec_send.shape[1]
    others = (0, 2, 6, 8, 1, 7, 3, 5)

    def inside(k):
        band = lat + k // 3 - 1
        return (band >= 0) & (band < n_lat)

    def peer(k):
        return (lat + k // 3 - 1, lax.rem(lon + k % 3 - 1 + n_lon, n_lon))

    def copy_of(stage, source, k):
        return pltpu.make_async_remote_copy(
            src_ref=source,
            dst_ref=landed.at[stage, 8 - k],
            send_sem=send_sem.at[stage, k],
            recv_sem=recv_sem.at[stage, 8 - k],
            device_id=peer(k),
            device_id_type=MESH,
        )

    def spread(stage, source):
        for k in others:

            @pl.when(inside(k))
            def _():
                copy_of(stage, source, k).start()

    def fold_out(stage, part, k):
        @pl.when((k != 4) & inside(k))
        def _():
            copy_of(stage, part_out.at[part, k], k).start()

    def arrived(stage, source):
        for k in others:

            @pl.when(inside(k))
            def _():
                copy_of(stage, source, 8 - k).wait_recv()

    def folded(stage, part):
        arrived(stage, part_out.at[part, 0])
        total = part_out[part, 4].astype(F32)
        for k in others:
            total = total + landed[stage, k].astype(F32)
        return total.astype(BF16)

    barrier = pltpu.get_barrier_semaphore()
    for k in others:

        @pl.when(inside(k))
        def _():
            pl.semaphore_signal(barrier, inc=1, device_id=peer(k), device_id_type=MESH)

    missing = jnp.where(lat == 0, 3, 0) + jnp.where(lat == n_lat - 1, 3, 0)
    pl.semaphore_wait(barrier, 8 - missing)

    spread(0, mesh_feat)

    for k in (0, 1, 2, 6, 7, 8):

        @pl.when(jnp.logical_not(inside(k)))
        def _():
            for stage in range(6):
                landed[stage, k] = jnp.zeros((mesh_rows, width), BF16)

    landed[0, 4] = mesh_feat[...]

    chunk = min(256, grid_rows)

    def rows_at(i, size):
        return pl.ds(pl.multiple_of(i * size, size), size)

    def project(i, _):
        rows = rows_at(i, chunk)
        enc_table[rows, :] = mm(grid_feat[rows, :], enc_src[...]).astype(BF16)
        dec_table[rows, :width] = mm(grid_feat[rows, :], dec_dst[...]).astype(BF16)
        dec_table[rows, width:] = mm_t(grid_cot[rows, :], dec_out[...]).astype(BF16)
        return 0

    lax.fori_loop(0, grid_rows // chunk, project, 0)

    def enc_gather(k, _):
        picks = pick_columns(column_of(enc_columns, k), grid_rows)
        enc_edges[rows_at(k, enc_cap), :] = mm(picks, enc_table[...]).astype(BF16)
        return 0

    lax.fori_loop(0, 9, enc_gather, 0)

    arrived(0, mesh_feat)

    def enc_forward(k, _):
        rows = rows_at(k, enc_cap)
        side = mm(landed[0, k], enc_dst[...])
        high = side.astype(BF16)
        low = (side - high.astype(F32)).astype(BF16)
        picks = pick_columns(column_of(enc_columns, k + 9), mesh_rows)
        near = mm(picks, high) + mm(picks, low)
        pre = enc_edges[rows, :].astype(F32) + near + enc_bias[...]
        gate = gate_of(pre)
        message = pre * gate
        enc_slope[rows, :] = gate + message * (1.0 - gate)
        targets = pick_rows(live_row(enc_recv, enc_count, k), mesh_rows)
        part_out[0, k] = mm(targets, message.astype(BF16)).astype(BF16)
        fold_out(1, 0, k)
        return 0

    lax.fori_loop(0, 9, enc_forward, 0)

    def dec_gather(k, _):
        picks = pick_columns(column_of(dec_columns, k + 9), grid_rows)
        dec_edges[rows_at(k, dec_cap), :] = mm(picks, dec_table[...]).astype(BF16)
        return 0

    lax.fori_loop(0, 5, dec_gather, 0)

    enc_sum = folded(1, 0)
    mesh_new = (mesh_feat[...].astype(F32) + mm(enc_sum, enc_out[...])).astype(BF16)
    dec_proj = mm(mesh_new, dec_src[...]).astype(BF16)
    tile_out[0] = dec_proj
    landed[2, 4] = dec_proj
    spread(2, tile_out.at[0])

    lax.fori_loop(5, 9, dec_gather, 0)

    arrived(2, tile_out.at[0])
    step = min(256, dec_cap)

    def dec_forward(k, _):
        near_picks = pick_columns(column_of(dec_columns, k), mesh_rows)
        near = landed[2, k]
        for first in range(0, dec_cap, step):
            rows = pl.ds(pl.multiple_of(k * dec_cap + first, step), step)
            pre = (
                mm(near_picks[first : first + step], near)
                + dec_edges[rows, :width].astype(F32)
                + dec_bias[...]
            )
            gate = gate_of(pre)
            message = pre * gate
            slope = gate + message * (1.0 - gate)
            back = dec_edges[rows, width:].astype(F32)
            dec_edges[rows, :width] = message.astype(BF16)
            dec_edges[rows, width:] = (back * slope).astype(BF16)
        targets = pick_rows(live_row(dec_send, dec_count, k), mesh_rows)
        part_out[1, k] = mm(targets, dec_edges[rows_at(k, dec_cap), width:]).astype(BF16)
        fold_out(3, 1, k)
        return 0

    lax.fori_loop(0, 9, dec_forward, 0)

    def dec_scatter(i, _):
        rows = rows_at(i, chunk)
        targets = jnp.concatenate(
            [pick_rows(live_row(dec_recv, dec_count, k), chunk, i * chunk) for k in range(9)], axis=1
        )
        summed = mm(targets, dec_edges[...]).astype(BF16)
        grid_new[rows, :] = (
            grid_feat[rows, :].astype(F32) + mm(summed[:, :width], dec_out[...])
        ).astype(BF16)
        grid_part[rows, :] = grid_cot[rows, :].astype(F32) + mm_t(summed[:, width:], dec_dst[...])
        return 0

    half = (grid_rows // chunk + 1) // 2
    lax.fori_loop(0, half, dec_scatter, 0)

    back = mm_t(folded(3, 1), dec_src[...])
    mesh_back[...] = back
    enc_back = mm_t(back.astype(BF16), enc_out[...]).astype(BF16)
    tile_out[1] = enc_back
    landed[4, 4] = enc_back
    spread(4, tile_out.at[1])

    lax.fori_loop(half, grid_rows // chunk, dec_scatter, 0)

    arrived(4, tile_out.at[1])

    def enc_backward(k, _):
        rows = rows_at(k, enc_cap)
        picks = pick_columns(column_of(enc_columns, k + 9), mesh_rows)
        grad = (mm(picks, landed[4, k]) * enc_slope[rows, :]).astype(BF16)
        enc_edges[rows, :] = grad
        targets = pick_rows(live_row(enc_recv, enc_count, k), mesh_rows)
        part_out[2, k] = mm(targets, grad).astype(BF16)
        fold_out(5, 2, k)
        return 0

    lax.fori_loop(0, 9, enc_backward, 0)

    def enc_scatter(i, _):
        rows = rows_at(i, chunk)
        targets = jnp.concatenate(
            [pick_rows(live_row(enc_send, enc_count, k), chunk, i * chunk) for k in range(9)], axis=1
        )
        summed = mm(targets, enc_edges[...]).astype(BF16)
        grid_grad[rows, :] = (grid_part[rows, :] + mm_t(summed, enc_src[...])).astype(BF16)
        return 0

    lax.fori_loop(0, grid_rows // chunk, enc_scatter, 0)

    mesh_grad[...] = (mesh_back[...] + mm_t(folded(5, 2), enc_dst[...])).astype(BF16)

    for k in others:

        @pl.when(inside(k))
        def _():
            copy_of(0, mesh_feat, k).wait_send()
            copy_of(1, part_out.at[0, k], k).wait_send()
            copy_of(2, tile_out.at[0], k).wait_send()
            copy_of(3, part_out.at[1, k], k).wait_send()
            copy_of(4, tile_out.at[1], k).wait_send()
            copy_of(5, part_out.at[2, k], k).wait_send()


def on_device(
    n_lat,
    n_lon,
    grid_feat,
    mesh_feat,
    enc_send,
    enc_recv,
    enc_count,
    dec_send,
    dec_recv,
    dec_count,
    enc_src,
    enc_dst,
    enc_bias,
    enc_out,
    dec_src,
    dec_dst,
    dec_bias,
    dec_out,
    grid_cot,
):
    grid_rows, width = grid_feat.shape
    mesh_rows = mesh_feat.shape[0]
    enc_slots = 9 * enc_send.shape[2]
    dec_slots = 9 * dec_send.shape[2]
    enc_columns = jnp.concatenate([enc_send[0], enc_recv[0]], axis=0).T.astype(F32)
    dec_columns = jnp.concatenate([dec_send[0], dec_recv[0]], axis=0).T.astype(F32)
    vmem = pl.BlockSpec(memory_space=pltpu.VMEM)
    smem = pl.BlockSpec(memory_space=pltpu.SMEM)
    return pl.pallas_call(
        functools.partial(kernel, n_lat, n_lon),
        out_shape=(
            jax.ShapeDtypeStruct((grid_rows, width), BF16),
            jax.ShapeDtypeStruct((mesh_rows, width), BF16),
            jax.ShapeDtypeStruct((grid_rows, width), BF16),
        ),
        in_specs=[vmem] * 4 + [smem] + [vmem] * 2 + [smem] + [vmem] * 11,
        out_specs=(vmem, vmem, vmem),
        scratch_shapes=[
            pltpu.VMEM((grid_rows, width), BF16),
            pltpu.VMEM((grid_rows, 2 * width), BF16),
            pltpu.VMEM((enc_slots, width), BF16),
            pltpu.VMEM((enc_slots, width), F32),
            pltpu.VMEM((dec_slots, 2 * width), BF16),
            pltpu.VMEM((grid_rows, width), F32),
            pltpu.VMEM((mesh_rows, width), F32),
            pltpu.VMEM((2, mesh_rows, width), BF16),
            pltpu.VMEM((3, 9, mesh_rows, width), BF16),
            pltpu.VMEM((6, 9, mesh_rows, width), BF16),
            pltpu.SemaphoreType.DMA((6, 9)),
            pltpu.SemaphoreType.DMA((6, 9)),
        ],
        compiler_params=pltpu.CompilerParams(
            collective_id=0, has_side_effects=True, vmem_limit_bytes=60 * 1024 * 1024
        ),
    )(
        grid_feat,
        mesh_feat,
        enc_send[0],
        enc_recv[0],
        enc_count,
        dec_send[0],
        dec_recv[0],
        dec_count,
        enc_columns,
        dec_columns,
        enc_src,
        enc_dst,
        enc_bias[None, :],
        enc_out,
        dec_src,
        dec_dst,
        dec_bias[None, :],
        dec_out,
        grid_cot,
    )


def solution(mesh):
    owned2 = P(("lat", "lon"), None)
    owned3 = P(("lat", "lon"), None, None)
    placed = (owned2, owned2, owned3, owned3, owned2, owned3, owned3, owned2) + (P(),) * 8 + (owned2,)
    return jax.shard_map(
        functools.partial(on_device, mesh.shape["lat"], mesh.shape["lon"]),
        mesh=mesh,
        in_specs=placed,
        out_specs=(owned2, owned2, owned2),
        check_vma=False,
    )
```

time: 229 us -> 86.4 us (0.38); the launches traced: 225 us -> 86.1 us
  Pallas kernels: 0 us -> 77.8 us
  local copies, waits for them, and re-layouts: 69.2 us -> 7.62 us
  matrix products: 49.8 us -> 0 us
  waiting for transfers between devices: 48.6 us -> 0 us
  starting transfers between devices: 32.8 us -> 0 us
  other arithmetic: 23.7 us -> 0.02 us
    pallas_call x0 -> x1, Pallas kernels: none -> 77.8 us  [on_device(): pl.pallas_call(functools.partial(kernel, n_lat, n_lon), out_shape=(jax.Sh...]
    gather x6 -> x0, local copies, waits for them, and re-layouts: 63.7 us -> none  [the longest x1 15.4 us: on_device(): grid_back[dec_grid_rows].astype(jnp.float32) * silu_slope(dec_pre)]
    dot_general x14 -> x0, matrix products: 49.8 us -> none  [the longest x1 12.7 us: on_device(): jnp.dot(dec_sum, dec_out, preferred_element_type=jnp.float32)]
    ppermute x24 -> x0, waiting for transfers between devices: 48.6 us -> none  [the longest x6 35 us: passed_along(): return lax.ppermute(array, axis, pairs)]
    ppermute x24 -> x0, starting transfers between devices: 32.8 us -> none  [the longest x6 16.5 us: passed_along(): return lax.ppermute(array, axis, pairs)]
    convert_element_type x4 -> x2, other arithmetic: 15.2 us -> 0.02 us  [the longest x1 0.01 us: on_device(): jnp.concatenate([dec_send[0], dec_recv[0]], axis=0).T.astype(F32)]
    unnamed x62 -> x21, local copies, waits for them, and re-layouts: 1.25 us -> 6 us
    add x5 -> x0, other arithmetic: 2.54 us -> none  [the longest x3 2.53 us: fold_home(): combined = framed[1] + lat_move(framed[0], -1) + lat_move(framed[2], 1)]
  transfers between devices with their start and end apart: 24 -> 0, of which waited for: 11 -> 0; matrix products, arithmetic and copies ran while one was open for 34% -> 0% of each run, Pallas kernels for 0% -> 0%
where the time goes in v1:
time: 86.4 us; the launch traced here: 86.1 us
  Pallas kernels  77.8 us (90%)
  local copies, waits for them, and re-layouts  7.62 us (9%)
    pallas_call x1, Pallas kernels, on_device(): pl.pallas_call(functools.partial(kernel, n_lat, n_lon), out_shape=(jax.Sh...  77.8 us
    unnamed x21, local copies, waits for them, and re-layouts  6 us

profile of v1, /device:TPU:13, one launch (start us, length us, event | category | flops | bytes accessed | tf_op | source)
XLA Modules:
  0.0 86.1 jit_solution(9036798621932893377)
XLA Ops:
  0.6 0.7 copy_bitcast_fusion.2
  1.4 0.0 copy-start.3
  1.4 0.0 copy-start.4
  1.4 0.0 copy-start.6
  1.4 0.0 copy-start.7
  1.4 0.6 copy-done.3
  1.9 0.0 copy-done.4
  2.0 0.1 copy-done.6
  2.1 0.0 copy-done.7
  2.1 0.0 copy-start.1
  2.1 0.0 copy-start.2
  2.2 0.6 copy-done.1
  2.7 0.0 copy-done.2
  2.7 0.8 copy.30
  3.5 0.8 copy.31
  4.4 77.8 %shard_map.184 = (bf16[1024,512]{1,0:T(8,128)(2,1)}, bf16[64,512]{1,0:T(8,128)(2,1)}, bf16[1024,512]{1,0:T(8,128)(2,1)}) custom-call(bf16[1024,512]{1,0:T(8,128)(2,1)} %grid_feat.1, bf16[64,512]{1,0:T(8,128)(2,1)} %mesh_feat.1, s32[9,256]{1,0:T(8,128)} %copy-done.4, s32[9,256]{1,0:T(8,128)} %copy-done.3, s32[1,9]{1,0:T(1,128)} %enc_count.1, ...), custom_call_target="tpu_custom_call" | custom-call | tf_op jit(solution)/shard_map/pallas_call | solution.py:340
  82.1 0.0 copy-start.5
  82.1 0.0 copy-start
  82.1 2.4 %copy.43 = bf16[1024,512]{1,0:T(8,128)(2,1)} copy(bf16[1024,512]{1,0:T(8,128)(2,1)} %get-tuple-element.10) | data formatting | bytes 2097152
  84.5 0.0 copy-done.5
  84.5 0.6 copy.44
  85.1 0.0 copy-done
  85.1 1.0 %copy.45 = bf16[1024,512]{1,0:T(8,128)(2,1)} copy(bf16[1024,512]{1,0:T(8,128)(2,1)S(1)} %copy-done) | data formatting | bytes 2097152
  (3 shorter events, 0.0 us)
Async XLA Ops:
  1.4 0.6 copy-start.3
  1.4 0.6 copy-start.4
  1.4 0.7 copy-start.6
  1.4 0.7 copy-start.7
  2.1 0.6 copy-start.1
  2.1 0.6 copy-start.2
  82.1 2.4 %copy-start.5 = (bf16[64,512]{1,0:T(8,128)(2,1)S(1)}, bf16[64,512]{1,0:T(8,128)(2,1)}, u32[]{:S(2)}) copy-start(bf16[64,512]{1,0:T(8,128)(2,1)} %get-tuple-element.11) | copy-start | bytes 196612
  82.1 3.0 %copy-start = (bf16[1024,512]{1,0:T(8,128)(2,1)S(1)}, bf16[1024,512]{1,0:T(8,128)(2,1)}, u32[]{:S(2)}) copy-start(bf16[1024,512]{1,0:T(8,128)(2,1)} %get-tuple-element.12) | copy-start | bytes 3145732

commit v2 on v1

--- a/solution.py
+++ b/solution.py
@@ -37,14 +37,21 @@
     return ones_where(rows == indices)
 
 
-def column_of(columns_ref, at):
-    columns = columns_ref[...]
+def lay_columns(index_ref, columns_ref, at):
+    blocks, _, slots = index_ref.shape
+    rows = [index_ref[k].astype(F32) for k in range(blocks)]
+    rows.append(jnp.zeros((16 - blocks, slots), F32))
+    columns_ref[at] = jnp.concatenate(rows, axis=0).T
+
+
+def column_of(columns_ref, which, at):
+    columns = columns_ref[which]
     lane = lax.broadcasted_iota(jnp.int32, columns.shape, 1)
     return jnp.sum(jnp.where(lane == at, columns, 0.0), axis=1, keepdims=True)
 
 
 def live_row(index_ref, count_ref, k):
-    indices = index_ref[pl.ds(k, 1), :]
+    indices = index_ref[k]
     return jnp.where(lane_row(indices.shape[1]) < count_ref[0, k], indices, -1)
 
 
@@ -63,8 +70,6 @@
     dec_send,
     dec_recv,
     dec_count,
-    enc_columns,
-    dec_columns,
     enc_src,
     enc_dst,
     enc_bias,
@@ -87,6 +92,8 @@
     tile_out,
     part_out,
     landed,
+    enc_columns,
+    dec_columns,
     send_sem,
     recv_sem,
 ):
@@ -94,9 +101,16 @@
     lon = lax.axis_index("lon")
     grid_rows, width = grid_feat.shape
     mesh_rows = mesh_feat.shape[0]
-    enc_cap = enc_send.shape[1]
-    dec_cap = dec_send.shape[1]
-    others = (0, 2, 6, 8, 1, 7, 3, 5)
+    enc_cap = enc_send.shape[2]
+    dec_cap = dec_send.shape[2]
+    turns = (4, 3, 5, 1, 7, 0, 2, 6, 8)
+    others = turns[1:]
+
+    def block_at(turn):
+        k = turns[0]
+        for i in range(1, 9):
+            k = jnp.where(turn == i, turns[i], k)
+        return k
 
     def inside(k):
         band = lat + k // 3 - 1
@@ -127,6 +141,11 @@
         def _():
             copy_of(stage, part_out.at[part, k], k).start()
 
+    def arrived_one(stage, source, k):
+        @pl.when((k != 4) & inside(k))
+        def _():
+            copy_of(stage, source, 8 - k).wait_recv()
+
     def arrived(stage, source):
         for k in others:
 
@@ -153,6 +172,11 @@
 
     spread(0, mesh_feat)
 
+    lay_columns(enc_send, enc_columns, 0)
+    lay_columns(enc_recv, enc_columns, 1)
+    lay_columns(dec_send, dec_columns, 0)
+    lay_columns(dec_recv, dec_columns, 1)
+
     for k in (0, 1, 2, 6, 7, 8):
 
         @pl.when(jnp.logical_not(inside(k)))
@@ -177,20 +201,20 @@
     lax.fori_loop(0, grid_rows // chunk, project, 0)
 
     def enc_gather(k, _):
-        picks = pick_columns(column_of(enc_columns, k), grid_rows)
+        picks = pick_columns(column_of(enc_columns, 0, k), grid_rows)
         enc_edges[rows_at(k, enc_cap), :] = mm(picks, enc_table[...]).astype(BF16)
         return 0
 
     lax.fori_loop(0, 9, enc_gather, 0)
 
-    arrived(0, mesh_feat)
-
-    def enc_forward(k, _):
+    def enc_forward(turn, _):
+        k = block_at(turn)
+        arrived_one(0, mesh_feat, k)
         rows = rows_at(k, enc_cap)
         side = mm(landed[0, k], enc_dst[...])
         high = side.astype(BF16)
         low = (side - high.astype(F32)).astype(BF16)
-        picks = pick_columns(column_of(enc_columns, k + 9), mesh_rows)
+        picks = pick_columns(column_of(enc_columns, 1, k), mesh_rows)
         near = mm(picks, high) + mm(picks, low)
         pre = enc_edges[rows, :].astype(F32) + near + enc_bias[...]
         gate = gate_of(pre)
@@ -204,7 +228,7 @@
     lax.fori_loop(0, 9, enc_forward, 0)
 
     def dec_gather(k, _):
-        picks = pick_columns(column_of(dec_columns, k + 9), grid_rows)
+        picks = pick_columns(column_of(dec_columns, 1, k), grid_rows)
         dec_edges[rows_at(k, dec_cap), :] = mm(picks, dec_table[...]).astype(BF16)
         return 0
 
@@ -219,11 +243,12 @@
 
     lax.fori_loop(5, 9, dec_gather, 0)
 
-    arrived(2, tile_out.at[0])
     step = min(256, dec_cap)
 
-    def dec_forward(k, _):
-        near_picks = pick_columns(column_of(dec_columns, k), mesh_rows)
+    def dec_forward(turn, _):
+        k = block_at(turn)
+        arrived_one(2, tile_out.at[0], k)
+        near_picks = pick_columns(column_of(dec_columns, 0, k), mesh_rows)
         near = landed[2, k]
         for first in range(0, dec_cap, step):
             rows = pl.ds(pl.multiple_of(k * dec_cap + first, step), step)
@@ -269,11 +294,11 @@
 
     lax.fori_loop(half, grid_rows // chunk, dec_scatter, 0)
 
-    arrived(4, tile_out.at[1])
-
-    def enc_backward(k, _):
+    def enc_backward(turn, _):
+        k = block_at(turn)
+        arrived_one(4, tile_out.at[1], k)
         rows = rows_at(k, enc_cap)
-        picks = pick_columns(column_of(enc_columns, k + 9), mesh_rows)
+        picks = pick_columns(column_of(enc_columns, 1, k), mesh_rows)
         grad = (mm(picks, landed[4, k]) * enc_slope[rows, :]).astype(BF16)
         enc_edges[rows, :] = grad
         targets = pick_rows(live_row(enc_recv, enc_count, k), mesh_rows)
@@ -333,8 +358,6 @@
     mesh_rows = mesh_feat.shape[0]
     enc_slots = 9 * enc_send.shape[2]
     dec_slots = 9 * dec_send.shape[2]
-    enc_columns = jnp.concatenate([enc_send[0], enc_recv[0]], axis=0).T.astype(F32)
-    dec_columns = jnp.concatenate([dec_send[0], dec_recv[0]], axis=0).T.astype(F32)
     vmem = pl.BlockSpec(memory_space=pltpu.VMEM)
     smem = pl.BlockSpec(memory_space=pltpu.SMEM)
     return pl.pallas_call(
@@ -344,7 +367,7 @@
             jax.ShapeDtypeStruct((mesh_rows, width), BF16),
             jax.ShapeDtypeStruct((grid_rows, width), BF16),
         ),
-        in_specs=[vmem] * 4 + [smem] + [vmem] * 2 + [smem] + [vmem] * 11,
+        in_specs=[vmem] * 4 + [smem] + [vmem] * 2 + [smem] + [vmem] * 9,
         out_specs=(vmem, vmem, vmem),
         scratch_shapes=[
             pltpu.VMEM((grid_rows, width), BF16),
@@ -357,6 +380,8 @@
             pltpu.VMEM((2, mesh_rows, width), BF16),
             pltpu.VMEM((3, 9, mesh_rows, width), BF16),
             pltpu.VMEM((6, 9, mesh_rows, width), BF16),
+            pltpu.VMEM((2, enc_send.shape[2], 16), F32),
+            pltpu.VMEM((2, dec_send.shape[2], 16), F32),
             pltpu.SemaphoreType.DMA((6, 9)),
             pltpu.SemaphoreType.DMA((6, 9)),
         ],
@@ -366,14 +391,12 @@
     )(
         grid_feat,
         mesh_feat,
-        enc_send[0],
-        enc_recv[0],
+        jnp.transpose(enc_send, (1, 0, 2)),
+        jnp.transpose(enc_recv, (1, 0, 2)),
         enc_count,
-        dec_send[0],
-        dec_recv[0],
+        jnp.transpose(dec_send, (1, 0, 2)),
+        jnp.transpose(dec_recv, (1, 0, 2)),
         dec_count,
-        enc_columns,
-        dec_columns,
         enc_src,
         enc_dst,
         enc_bias[None, :],

time: 86.4 us -> 75.8 us (0.88)
  the two profiles are of different devices: /device:TPU:13 before, /device:TPU:25 now
where the time goes in v2:
time: 75.8 us; the launch traced here: 75.7 us
  Pallas kernels  71 us (94%)
  local copies, waits for them, and re-layouts  3.96 us (5%)
    pallas_call x1, Pallas kernels, on_device(): pl.pallas_call(functools.partial(kernel, n_lat, n_lon), out_shape=(jax.Sh...  71 us
    unnamed x7, local copies, waits for them, and re-layouts  3.96 us

profile of v2, /device:TPU:25, one launch (start us, length us, event | category | flops | bytes accessed | tf_op | source)
XLA Modules:
  0.0 75.7 jit_solution(1657066828160367029)
XLA Ops:
  0.6 71.0 %shard_map.184 = (bf16[1024,512]{1,0:T(8,128)(2,1)}, bf16[64,512]{1,0:T(8,128)(2,1)}, bf16[1024,512]{1,0:T(8,128)(2,1)}) custom-call(bf16[1024,512]{1,0:T(8,128)(2,1)} %grid_feat.1, bf16[64,512]{1,0:T(8,128)(2,1)} %mesh_feat.1, s32[9,1,256]{2,1,0:T(1,128)} %bitcast.8, s32[9,1,256]{2,1,0:T(1,128)} %bitcast.9, s32[1,9]{1,0:T(1,128)} %enc_count.1, ...), custom_call_target="tpu_custom_call" | custom-call | tf_op jit(solution)/shard_map/pallas_call | solution.py:363
  71.7 0.0 copy-start.1
  71.7 0.0 copy-start
  71.7 2.4 %copy.23 = bf16[1024,512]{1,0:T(8,128)(2,1)} copy(bf16[1024,512]{1,0:T(8,128)(2,1)} %get-tuple-element.6) | data formatting | bytes 2097152
  74.1 0.0 copy-done.1
  74.1 0.6 copy.24
  74.7 0.0 copy-done
  74.7 1.0 %copy.25 = bf16[1024,512]{1,0:T(8,128)(2,1)} copy(bf16[1024,512]{1,0:T(8,128)(2,1)S(1)} %copy-done) | data formatting | bytes 2097152
Async XLA Ops:
  71.7 2.4 %copy-start.1 = (bf16[64,512]{1,0:T(8,128)(2,1)S(1)}, bf16[64,512]{1,0:T(8,128)(2,1)}, u32[]{:S(2)}) copy-start(bf16[64,512]{1,0:T(8,128)(2,1)} %get-tuple-element.7) | copy-start | bytes 196612
  71.7 3.0 %copy-start = (bf16[1024,512]{1,0:T(8,128)(2,1)S(1)}, bf16[1024,512]{1,0:T(8,128)(2,1)}, u32[]{:S(2)}) copy-start(bf16[1024,512]{1,0:T(8,128)(2,1)} %get-tuple-element.8) | copy-start | bytes 3145732

commit v3 on v2

--- a/solution.py
+++ b/solution.py
@@ -130,11 +130,27 @@
         )
 
     def spread(stage, source):
-        for k in others:
+        for k in (1, 7, 3, 5):
 
             @pl.when(inside(k))
             def _():
                 copy_of(stage, source, k).start()
+
+    def pass_on(stage, source):
+        for k in (1, 7):
+
+            @pl.when(inside(k))
+            def _():
+                copy_of(stage, source, 8 - k).wait_recv()
+                for corner, side in ((k - 1, 1), (k + 1, n_lon - 1)):
+                    pltpu.make_async_remote_copy(
+                        src_ref=landed.at[stage, k],
+                        dst_ref=landed.at[stage, corner],
+                        send_sem=send_sem.at[stage, corner],
+                        recv_sem=recv_sem.at[stage, corner],
+                        device_id=(lat, lax.rem(lon + side, n_lon)),
+                        device_id_type=MESH,
+                    ).start()
 
     def fold_out(stage, part, k):
         @pl.when((k != 4) & inside(k))
@@ -142,7 +158,7 @@
             copy_of(stage, part_out.at[part, k], k).start()
 
     def arrived_one(stage, source, k):
-        @pl.when((k != 4) & inside(k))
+        @pl.when((k != 4) & (k != 1) & (k != 7) & inside(k))
         def _():
             copy_of(stage, source, 8 - k).wait_recv()
 
@@ -225,6 +241,7 @@
         fold_out(1, 0, k)
         return 0
 
+    pass_on(0, mesh_feat)
     lax.fori_loop(0, 9, enc_forward, 0)
 
     def dec_gather(k, _):
@@ -268,6 +285,7 @@
         fold_out(3, 1, k)
         return 0
 
+    pass_on(2, tile_out.at[0])
     lax.fori_loop(0, 9, dec_forward, 0)
 
     def dec_scatter(i, _):
@@ -292,7 +310,8 @@
     landed[4, 4] = enc_back
     spread(4, tile_out.at[1])
 
-    lax.fori_loop(half, grid_rows // chunk, dec_scatter, 0)
+    most = (half + grid_rows // chunk) // 2
+    lax.fori_loop(half, most, dec_scatter, 0)
 
     def enc_backward(turn, _):
         k = block_at(turn)
@@ -306,6 +325,7 @@
         fold_out(5, 2, k)
         return 0
 
+    pass_on(4, tile_out.at[1])
     lax.fori_loop(0, 9, enc_backward, 0)
 
     def enc_scatter(i, _):
@@ -317,6 +337,7 @@
         grid_grad[rows, :] = (grid_part[rows, :] + mm_t(summed, enc_src[...])).astype(BF16)
         return 0
 
+    lax.fori_loop(most, grid_rows // chunk, dec_scatter, 0)
     lax.fori_loop(0, grid_rows // chunk, enc_scatter, 0)
 
     mesh_grad[...] = (mesh_back[...] + mm_t(folded(5, 2), enc_dst[...])).astype(BF16)

time: 75.8 us -> 70.6 us (0.931)
  the two profiles are of different devices: /device:TPU:25 before, /device:TPU:13 now
where the time goes in v3:
time: 70.6 us; the launch traced here: 70.5 us
  Pallas kernels  65.9 us (93%)
  local copies, waits for them, and re-layouts  3.96 us (6%)
    pallas_call x1, Pallas kernels, on_device(): pl.pallas_call(functools.partial(kernel, n_lat, n_lon), out_shape=(jax.Sh...  65.9 us
    unnamed x7, local copies, waits for them, and re-layouts  3.96 us

profile of v3, /device:TPU:13, one launch (start us, length us, event | category | flops | bytes accessed | tf_op | source)
XLA Modules:
  0.0 70.5 jit_solution(8933221863669965871)
XLA Ops:
  0.6 65.9 %shard_map.184 = (bf16[1024,512]{1,0:T(8,128)(2,1)}, bf16[64,512]{1,0:T(8,128)(2,1)}, bf16[1024,512]{1,0:T(8,128)(2,1)}) custom-call(bf16[1024,512]{1,0:T(8,128)(2,1)} %grid_feat.1, bf16[64,512]{1,0:T(8,128)(2,1)} %mesh_feat.1, s32[9,1,256]{2,1,0:T(1,128)} %bitcast.8, s32[9,1,256]{2,1,0:T(1,128)} %bitcast.9, s32[1,9]{1,0:T(1,128)} %enc_count.1, ...), custom_call_target="tpu_custom_call" | custom-call | tf_op jit(solution)/shard_map/pallas_call | solution.py:384
  66.5 0.0 copy-start.1
  66.5 0.0 copy-start
  66.5 2.4 %copy.23 = bf16[1024,512]{1,0:T(8,128)(2,1)} copy(bf16[1024,512]{1,0:T(8,128)(2,1)} %get-tuple-element.6) | data formatting | bytes 2097152
  68.9 0.0 copy-done.1
  68.9 0.6 copy.24
  69.5 0.0 copy-done
  69.5 1.0 %copy.25 = bf16[1024,512]{1,0:T(8,128)(2,1)} copy(bf16[1024,512]{1,0:T(8,128)(2,1)S(1)} %copy-done) | data formatting | bytes 2097152
Async XLA Ops:
  66.5 2.4 %copy-start.1 = (bf16[64,512]{1,0:T(8,128)(2,1)S(1)}, bf16[64,512]{1,0:T(8,128)(2,1)}, u32[]{:S(2)}) copy-start(bf16[64,512]{1,0:T(8,128)(2,1)} %get-tuple-element.7) | copy-start | bytes 196612
  66.5 3.0 %copy-start = (bf16[1024,512]{1,0:T(8,128)(2,1)S(1)}, bf16[1024,512]{1,0:T(8,128)(2,1)}, u32[]{:S(2)}) copy-start(bf16[1024,512]{1,0:T(8,128)(2,1)} %get-tuple-element.8) | copy-start | bytes 3145732

commit v4 on v3

--- a/solution.py
+++ b/solution.py
@@ -354,6 +354,24 @@
             copy_of(5, part_out.at[2, k], k).wait_send()
 
 
+def settle(*refs):
+    for source, target in zip(refs[:3], refs[3:]):
+        target[...] = source[...]
+
+
+def written_out(results, parts):
+    blocks = [
+        pl.BlockSpec((r.shape[0] // parts, r.shape[1]), lambda i: (i, 0)) for r in results
+    ]
+    return pl.pallas_call(
+        settle,
+        grid=(parts,),
+        out_shape=tuple(jax.ShapeDtypeStruct(r.shape, r.dtype) for r in results),
+        in_specs=blocks,
+        out_specs=tuple(blocks),
+    )(*results)
+
+
 def on_device(
     n_lat,
     n_lon,
@@ -381,7 +399,7 @@
     dec_slots = 9 * dec_send.shape[2]
     vmem = pl.BlockSpec(memory_space=pltpu.VMEM)
     smem = pl.BlockSpec(memory_space=pltpu.SMEM)
-    return pl.pallas_call(
+    results = pl.pallas_call(
         functools.partial(kernel, n_lat, n_lon),
         out_shape=(
             jax.ShapeDtypeStruct((grid_rows, width), BF16),
@@ -428,6 +446,7 @@
         dec_out,
         grid_cot,
     )
+    return written_out(results, 4)
 
 
 def solution(mesh):

time: 70.6 us -> 70.5 us (level)
  local copies, waits for them, and re-layouts: 3.96 us -> 0 us
  Pallas kernels: 65.9 us -> 69.7 us
    unnamed x7 -> x0, local copies, waits for them, and re-layouts: 3.96 us -> none
    pallas_call x0 -> x1, Pallas kernels: none -> 3.8 us  [written_out(): pl.pallas_call(settle, grid=(parts,), out_shape=tuple((jax.ShapeDtypeStru...]
where the time goes in v4:
time: 70.5 us; the launch traced here: 70.3 us
  Pallas kernels  69.7 us (99%)
    pallas_call x1, Pallas kernels, on_device(): pl.pallas_call(functools.partial(kernel, n_lat, n_lon), out_shape=(jax.Sh...  65.9 us
    pallas_call x1, Pallas kernels, written_out(): pl.pallas_call(settle, grid=(parts,), out_shape=tuple((jax.ShapeDtypeStru...  3.8 us

profile of v4, /device:TPU:13, one launch (start us, length us, event | category | flops | bytes accessed | tf_op | source)
XLA Modules:
  0.0 70.3 jit_solution(6799582513724350953)
XLA Ops:
  0.6 65.9 %shard_map.184 = (bf16[1024,512]{1,0:T(8,128)(2,1)}, bf16[64,512]{1,0:T(8,128)(2,1)}, bf16[1024,512]{1,0:T(8,128)(2,1)}) custom-call(bf16[1024,512]{1,0:T(8,128)(2,1)} %grid_feat.1, bf16[64,512]{1,0:T(8,128)(2,1)} %mesh_feat.1, s32[9,1,256]{2,1,0:T(1,128)} %bitcast.8, s32[9,1,256]{2,1,0:T(1,128)} %bitcast.9, s32[1,9]{1,0:T(1,128)} %enc_count.1, ...), custom_call_target="tpu_custom_call" | custom-call | tf_op jit(solution)/shard_map/pallas_call | solution.py:402
  66.5 3.8 %shard_map.185 = (bf16[1024,512]{1,0:T(8,128)(2,1)}, bf16[64,512]{1,0:T(8,128)(2,1)}, bf16[1024,512]{1,0:T(8,128)(2,1)}) custom-call(bf16[1024,512]{1,0:T(8,128)(2,1)} %get-tuple-element.6.refs_0_, bf16[64,512]{1,0:T(8,128)(2,1)} %get-tuple-element.7.refs_1_, bf16[1024,512]{1,0:T(8,128)(2,1)} %get-tuple-element.8.refs_2_), custom_call_target="tpu_custom_call" | custom-call | tf_op jit(solution)/shard_map/pallas_call | solution.py:366
